TPU v7x, 32 devices: a whole 2x2x4 slice. The times are simulated.
32 devices in a mesh: dp: 4 (over y, x), tensor: 8 (over z, core).
Axes of the slice: x: 2, y: 2, z: 4, core: 2. Of those that a mesh axis runs over, the one named last changes fastest.
Arguments:
- inputs: bfloat16 [16384, 2048], P(('dp', 'tensor')), may hold values from -6 to 6
- block_ids: int32 [16, 1024], P('dp'), may hold values from 0 to 4, never falling along the last dimension, each value on 1 to 256 neighbouring positions
- norm_gain: bfloat16 [2048], replicated, may hold values from 0.5 to 1.5
- norm_bias: bfloat16 [2048], replicated, may hold values from -3 to 3
- query_weight: bfloat16 [2048, 2048], P('dp', 'tensor'), may hold values from -0.125 to 0.125
- query_bias: bfloat16 [2048], P('tensor'), may hold values from -3 to 3
- key_weight: bfloat16 [2048, 2048], P('dp', 'tensor'), may hold values from -0.125 to 0.125
- key_bias: bfloat16 [2048], P('tensor'), may hold values from -3 to 3
- value_weight: bfloat16 [2048, 2048], P('dp', 'tensor'), may hold values from -0.125 to 0.125
- value_bias: bfloat16 [2048], P('tensor'), may hold values from -3 to 3
- out_weight: bfloat16 [2048, 2048], P('tensor', 'dp'), may hold values from -3 to 3
- out_bias: bfloat16 [2048], replicated, may hold values from -3 to 3
- up_weight: bfloat16 [2048, 8192], P('dp', 'tensor'), may hold values from -0.125 to 0.125
- up_bias: bfloat16 [8192], P('tensor'), may hold values from -3 to 3
- down_weight: bfloat16 [8192, 2048], P('tensor', 'dp'), may hold values from -0.09375 to 0.09375
- down_bias: bfloat16 [2048], replicated, may hold values from -3 to 3
- grad_out: bfloat16 [16384, 2048], P(('dp', 'tensor')), may hold values from -6 to 6
Outputs:
- output: bfloat16 [16384, 2048], P(('dp', 'tensor'))
- input_grad: bfloat16 [16384, 2048], P(('dp', 'tensor'))
- norm_gain_grad: float32 [2048], replicated
- norm_bias_grad: float32 [2048], replicated
- query_weight_grad: float32 [2048, 2048], P('dp', 'tensor')
- query_bias_grad: float32 [2048], P('tensor')
- key_weight_grad: float32 [2048, 2048], P('dp', 'tensor')
- key_bias_grad: float32 [2048], P('tensor')
- value_weight_grad: float32 [2048, 2048], P('dp', 'tensor')
- value_bias_grad: float32 [2048], P('tensor')
- out_weight_grad: float32 [2048, 2048], P('tensor', 'dp')
- out_bias_grad: float32 [2048], replicated
- up_weight_grad: float32 [2048, 8192], P('dp', 'tensor')
- up_bias_grad: float32 [8192], P('tensor')
- down_weight_grad: float32 [8192, 2048], P('tensor', 'dp')
- down_bias_grad: float32 [2048], replicated
Inputs may be any that keep to these rules, and one draw needn't show every extreme that they name: `block_ids`: in each sequence the block numbers never fall along the positions; a block spans 1 to 256 positions, and one block of each sequence spans exactly 256.
All inputs are finite; a program needn't handle non-finite values.
Results may differ from a plain program's by a relative error of at most 0.012.
The roundings to bfloat16 on the way count: a program that leaves them out, or rounds other values in their place, can miss the bound.
Values may be sent and summed in bfloat16 or wider, within the bound.
A program may use at most 320 MiB of HBM per device.

v0:
```python
import jax
import jax.numpy as jnp
from jax import lax
from jax.sharding import PartitionSpec as P

HEAD_DIM = 64
ROT = 32
eps_norm = 1e-05


def normalize(values, gain_in, shift_in):
    center = jnp.mean(values, axis=-1, keepdims=True)
    centered = values - center
    variance = jnp.mean(centered * centered, axis=-1, keepdims=True)
    return centered * lax.rsqrt(variance + eps_norm) * gain_in + shift_in


def rotary_tables(length, rot_width):
    halves = rot_width // 2
    exponent = jnp.arange(halves, dtype=jnp.float32) * (2.0 / rot_width)
    frequency = jnp.power(10000.0, -exponent)
    angles = jnp.arange(length, dtype=jnp.float32)[:, None] * frequency[None, :]
    angles = jnp.concatenate([angles, angles], axis=1)
    return (jnp.cos(angles), jnp.sin(angles))


def rotate(per_head, cos_table, sin_table):
    rot_width = cos_table.shape[-1]
    halves = rot_width // 2
    first_half = per_head[..., :halves]
    second_half = per_head[..., halves:rot_width]
    turned = jnp.concatenate([-second_half, first_half], axis=-1)
    rotated = per_head[..., :rot_width] * cos_table[:, None, :] + turned * sin_table[:, None, :]
    return jnp.concatenate([rotated, per_head[..., rot_width:]], axis=-1)


def masked_scores(query_block, key_block, query_ids, key_ids):
    raw_scores = jnp.einsum(
        "qhd,khd->hqk", query_block, key_block, preferred_element_type=jnp.float32
    ) * HEAD_DIM ** (-0.5)
    allowed = key_ids[None, None, :] <= query_ids[None, :, None]
    return jnp.where(allowed, raw_scores, -1000000000.0)


def gelu_tanh(values):
    return jax.nn.gelu(values, approximate=True)


def per_device(
    inputs,
    block_ids,
    norm_gain,
    norm_bias,
    query_weight,
    query_bias,
    key_weight,
    key_bias,
    value_weight,
    value_bias,
    out_weight,
    out_bias,
    up_weight,
    up_bias,
    down_weight,
    down_bias,
    grad_out,
):
    seq_count, length = block_ids.shape
    local_width = query_weight.shape[1]
    local_heads = local_width // HEAD_DIM
    block_rows = min(512, length)
    per_sequence = length // block_rows
    all_rows = seq_count * length
    score_scale = HEAD_DIM ** (-0.5)
    gain_float = norm_gain.astype(jnp.float32)
    shift_float = norm_bias.astype(jnp.float32)
    inputs_float = inputs.astype(jnp.float32)
    normed = normalize(inputs_float, gain_float, shift_float).astype(jnp.bfloat16)
    full_query, full_key, full_value, full_up, full_out, full_down = (
        lax.all_gather(query_weight, "dp", axis=0, tiled=True),
        lax.all_gather(key_weight, "dp", axis=0, tiled=True),
        lax.all_gather(value_weight, "dp", axis=0, tiled=True),
        lax.all_gather(up_weight, "dp", axis=0, tiled=True),
        lax.all_gather(out_weight, "dp", axis=1, tiled=True),
        lax.all_gather(down_weight, "dp", axis=1, tiled=True),
    )
    group_rows = lax.all_gather(normed, "tensor", axis=0, tiled=True)
    cos_table, sin_table = rotary_tables(length, ROT)

    def project(weight_part, bias_part):
        return jnp.dot(
            group_rows, weight_part, preferred_element_type=jnp.float32
        ) + bias_part.astype(jnp.float32)

    def split_heads(values):
        return values.reshape(seq_count, length, local_heads, HEAD_DIM)

    queries = rotate(split_heads(project(full_query, query_bias)), cos_table, sin_table).astype(
        jnp.bfloat16
    )
    key_rows = rotate(split_heads(project(full_key, key_bias)), cos_table, sin_table).astype(
        jnp.bfloat16
    )
    value_rows = split_heads(project(full_value, value_bias)).astype(jnp.bfloat16)

    def forward_block(block_index):
        sequence = block_index // per_sequence
        offset = block_index % per_sequence * block_rows
        seq_ids = block_ids[sequence]
        query_block = lax.dynamic_slice_in_dim(queries[sequence], offset, block_rows, 0)
        query_ids = lax.dynamic_slice_in_dim(seq_ids, offset, block_rows, 0)
        scores = masked_scores(query_block, key_rows[sequence], query_ids, seq_ids)
        highest = jnp.max(scores, axis=2, keepdims=True)
        shifted = jnp.exp(scores - highest)
        totals = jnp.sum(shifted, axis=2, keepdims=True)
        weights_low = (shifted / totals).astype(jnp.bfloat16)
        mixed_rows = jnp.einsum(
            "hqk,khd->qhd", weights_low, value_rows[sequence], preferred_element_type=jnp.float32
        )
        return (mixed_rows, (highest + jnp.log(totals))[:, :, 0])

    attended, log_sums = lax.map(forward_block, jnp.arange(seq_count * per_sequence))
    attended_low = attended.reshape(all_rows, local_width).astype(jnp.bfloat16)
    hidden = project(full_up, up_bias)
    active = gelu_tanh(hidden).astype(jnp.bfloat16)
    branch_rows = lax.psum_scatter(
        jnp.dot(attended_low, full_out, preferred_element_type=jnp.float32)
        + jnp.dot(active, full_down, preferred_element_type=jnp.float32),
        "tensor",
        scatter_dimension=0,
        tiled=True,
    )
    output = (
        inputs_float + branch_rows + out_bias.astype(jnp.float32) + down_bias.astype(jnp.float32)
    ).astype(jnp.bfloat16)
    back_query, back_key, back_value, back_up, back_out, back_down = (
        lax.all_gather(query_weight, "dp", axis=0, tiled=True),
        lax.all_gather(key_weight, "dp", axis=0, tiled=True),
        lax.all_gather(value_weight, "dp", axis=0, tiled=True),
        lax.all_gather(up_weight, "dp", axis=0, tiled=True),
        lax.all_gather(out_weight, "dp", axis=1, tiled=True),
        lax.all_gather(down_weight, "dp", axis=1, tiled=True),
    )
    back_rows = lax.all_gather(normed, "tensor", axis=0, tiled=True)
    upstream = lax.all_gather(grad_out, "tensor", axis=0, tiled=True)
    out_wgrad = jnp.einsum("rk,rd->kd", attended_low, upstream, preferred_element_type=jnp.float32)
    down_wgrad = jnp.einsum("rf,rd->fd", active, upstream, preferred_element_type=jnp.float32)
    attended_grad = jnp.einsum(
        "rd,kd->rk", upstream, back_out, preferred_element_type=jnp.float32
    ).astype(jnp.bfloat16)
    active_grad = jnp.einsum("rd,fd->rf", upstream, back_down, preferred_element_type=jnp.float32)
    unused_value, gelu_pull = jax.vjp(gelu_tanh, hidden)
    hidden_grad = gelu_pull(active_grad)[0].astype(jnp.bfloat16)
    grad_heads = split_heads(attended_grad)
    sums_grouped = log_sums.reshape(seq_count, per_sequence, local_heads, block_rows)

    def backward_sequence(sequence):
        seq_ids = block_ids[sequence]
        seq_queries = queries[sequence]
        seq_keys = key_rows[sequence]
        seq_values = value_rows[sequence]
        seq_grads = grad_heads[sequence]
        seq_sums = sums_grouped[sequence]

        def backward_block(running, block_number):
            key_total, value_total = running
            offset = block_number * block_rows
            query_block = lax.dynamic_slice_in_dim(seq_queries, offset, block_rows, 0)
            query_ids = lax.dynamic_slice_in_dim(seq_ids, offset, block_rows, 0)
            grad_block = lax.dynamic_slice_in_dim(seq_grads, offset, block_rows, 0)
            scores = masked_scores(query_block, seq_keys, query_ids, seq_ids)
            prob_rows = jnp.exp(scores - seq_sums[block_number][:, :, None])
            value_total = value_total + jnp.einsum(
                "hqk,qhd->khd",
                prob_rows.astype(jnp.bfloat16),
                grad_block,
                preferred_element_type=jnp.float32,
            )
            prob_grad = jnp.einsum(
                "qhd,khd->hqk", grad_block, seq_values, preferred_element_type=jnp.float32
            )
            row_inner = jnp.sum(prob_grad * prob_rows, axis=2, keepdims=True)
            score_grad = (prob_rows * (prob_grad - row_inner)).astype(jnp.bfloat16)
            query_part = (
                jnp.einsum("hqk,khd->qhd", score_grad, seq_keys, preferred_element_type=jnp.float32)
                * score_scale
            )
            key_total = (
                key_total
                + jnp.einsum(
                    "hqk,qhd->khd", score_grad, query_block, preferred_element_type=jnp.float32
                )
                * score_scale
            )
            return ((key_total, value_total), query_part)

        zero_total = jnp.zeros((length, local_heads, HEAD_DIM), jnp.float32)
        (key_total, value_total), query_parts = lax.scan(
            backward_block, (zero_total, zero_total), jnp.arange(per_sequence)
        )
        return (query_parts.reshape(length, local_heads, HEAD_DIM), key_total, value_total)

    query_grad_rot, key_grad_rot, value_grad_all = lax.map(backward_sequence, jnp.arange(seq_count))
    query_grad = (
        rotate(query_grad_rot, cos_table, -sin_table)
        .reshape(all_rows, local_width)
        .astype(jnp.bfloat16)
    )
    key_grad = (
        rotate(key_grad_rot, cos_table, -sin_table)
        .reshape(all_rows, local_width)
        .astype(jnp.bfloat16)
    )
    value_grad = value_grad_all.reshape(all_rows, local_width).astype(jnp.bfloat16)
    query_wgrad = jnp.einsum("rd,rk->dk", back_rows, query_grad, preferred_element_type=jnp.float32)
    key_wgrad = jnp.einsum("rd,rk->dk", back_rows, key_grad, preferred_element_type=jnp.float32)
    value_wgrad = jnp.einsum("rd,rk->dk", back_rows, value_grad, preferred_element_type=jnp.float32)
    up_wgrad = jnp.einsum("rd,rf->df", back_rows, hidden_grad, preferred_element_type=jnp.float32)
    normed_grad = lax.psum_scatter(
        jnp.einsum("rk,dk->rd", query_grad, back_query, preferred_element_type=jnp.float32)
        + jnp.einsum("rk,dk->rd", key_grad, back_key, preferred_element_type=jnp.float32)
        + jnp.einsum("rk,dk->rd", value_grad, back_value, preferred_element_type=jnp.float32)
        + jnp.einsum("rf,df->rd", hidden_grad, back_up, preferred_element_type=jnp.float32),
        "tensor",
        scatter_dimension=0,
        tiled=True,
    )
    unused_norm, norm_pull = jax.vjp(normalize, inputs_float, gain_float, shift_float)
    input_part, gain_part, shift_part = norm_pull(normed_grad)
    input_grad = (grad_out.astype(jnp.float32) + input_part).astype(jnp.bfloat16)
    bias_part = jnp.sum(grad_out, axis=0, dtype=jnp.float32)
    gain_grad, shift_grad, outer_bias_grad = lax.psum(
        (gain_part, shift_part, bias_part), ("dp", "tensor")
    )
    query_bias_grad, key_bias_grad, value_bias_grad, up_bias_grad = lax.psum(
        (
            jnp.sum(query_grad, axis=0, dtype=jnp.float32),
            jnp.sum(key_grad, axis=0, dtype=jnp.float32),
            jnp.sum(value_grad, axis=0, dtype=jnp.float32),
            jnp.sum(hidden_grad, axis=0, dtype=jnp.float32),
        ),
        "dp",
    )
    (
        query_weight_grad,
        key_weight_grad,
        value_weight_grad,
        up_weight_grad,
        out_weight_grad,
        down_weight_grad,
    ) = (
        lax.psum_scatter(query_wgrad, "dp", scatter_dimension=0, tiled=True),
        lax.psum_scatter(key_wgrad, "dp", scatter_dimension=0, tiled=True),
        lax.psum_scatter(value_wgrad, "dp", scatter_dimension=0, tiled=True),
        lax.psum_scatter(up_wgrad, "dp", scatter_dimension=0, tiled=True),
        lax.psum_scatter(out_wgrad, "dp", scatter_dimension=1, tiled=True),
        lax.psum_scatter(down_wgrad, "dp", scatter_dimension=1, tiled=True),
    )
    return (
        output,
        input_grad,
        gain_grad,
        shift_grad,
        query_weight_grad,
        query_bias_grad,
        key_weight_grad,
        key_bias_grad,
        value_weight_grad,
        value_bias_grad,
        out_weight_grad,
        outer_bias_grad,
        up_weight_grad,
        up_bias_grad,
        down_weight_grad,
        outer_bias_grad,
    )


def solution(mesh):
    return jax.shard_map(
        per_device,
        mesh=mesh,
        in_specs=(
            P(("dp", "tensor"), None),
            P("dp", None),
            P(),
            P(),
            P("dp", "tensor"),
            P("tensor"),
            P("dp", "tensor"),
            P("tensor"),
            P("dp", "tensor"),
            P("tensor"),
            P("tensor", "dp"),
            P(),
            P("dp", "tensor"),
            P("tensor"),
            P("tensor", "dp"),
            P(),
            P(("dp", "tensor"), None),
        ),
        out_specs=(
            P(("dp", "tensor"), None),
            P(("dp", "tensor"), None),
            P(),
            P(),
            P("dp", "tensor"),
            P("tensor"),
            P("dp", "tensor"),
            P("tensor"),
            P("dp", "tensor"),
            P("tensor"),
            P("tensor", "dp"),
            P(),
            P("dp", "tensor"),
            P("tensor"),
            P("tensor", "dp"),
            P(),
        ),
        check_vma=False,
    )
```

profile of v0, /device:TPU:0, one launch (start us, length us, event | category | flops | bytes accessed | tf_op | source)
XLA Modules:
  0.0 2073.4 jit_solution(4787446761198307838)
XLA Ops:
  22.7 16.5 all-gather.15.cloned.1.call-done
  39.2 153.3 %all-gather.9.cloned.1.call-done = bf16[4096,2048]{1,0:T(8,128)(2,1)} async-done(((bf16[512,2048]{1,0:T(8,128)(2,1)}), bf16[4096,2048]{1,0:T(8,128)(2,1)}) %all-gather.9.cloned.1.call-update) | async-done | bytes 16777232 | tf_op jit(solution)/shard_map/all_gather | solution.py:87
  192.5 12.6 convolution_add_fusion.1
  205.1 5.8 copy.54
  210.9 6.1 reshape.272
  222.3 12.6 convolution_add_fusion.2
  234.8 5.7 copy.53
  240.5 6.2 reshape.271
  248.8 3.6 slice_negate_fusion.1
  252.4 12.1 fusion.53
  264.6 7.1 reshape.277
  271.7 6.9 copy.55
  278.6 149.8 %all-gather.23.cloned.1.call-done = bf16[4096,2048]{1,0:T(8,128)(2,1)} async-done(((bf16[512,2048]{1,0:T(8,128)(2,1)}), bf16[4096,2048]{1,0:T(8,128)(2,1)}) %all-gather.23.cloned.1.call-update) | async-done | bytes 16777232 | tf_op jit(solution)/shard_map/all_gather | solution.py:145
  428.4 11.9 convolution_convert_fusion
  440.3 7.4 reshape.276
  447.8 7.0 copy.63
  454.7 4.7 fusion.66
  466.2 102.8 %while.44 = (s32[]{:T(128)}, bf16[8,512,4,64]{1,3,2,0:T(8,128)(2,1)S(1)}, f32[8,4,512]{2,1,0:T(4,128)S(1)}, s32[8]{0:T(128)S(1)}, bf16[4,1024,4,64]{1,3,2,0:T(8,...) while((s32[]{:T(128)}, ...), condition=%wide.region_5.6_spmd, body=%wide.region_2.5_spmd.sunk | while | flops 562558976 | bytes 29182452 | solution.py:122
  475.4 3.6 fusion.148
  488.2 3.6 fusion.148
  501.1 3.6 fusion.148
  513.9 3.7 fusion.148
  526.8 3.6 fusion.148
  539.6 3.6 fusion.148
  552.5 3.6 fusion.148
  565.3 3.6 fusion.148
  570.3 342.7 %while.46 = (s32[]{:T(128)}, f32[4,1024,4,64]{1,0,3,2:T(4,128)}, f32[4,1024,4,64]{1,0,3,2:T(4,128)}, bf16[4,1024,4,64]{1,3,2,0:T(8,128)(2,1)}, s32[4]{0:T(128)S(...) while((s32[]{:T(128)}, f32[4,1024,4,64]{1,0,3,2:T(4,128)}, ...), condition=%wide.region_11.12_spmd, body=%wide.region_7.11_spmd.sunk | while | flops 1375598592 | bytes 110209856 | solution.py:203
  575.7 33.3 %while.47 = (s32[]{:T(128)}, f32[1024,4,64]{0,2,1:T(8,128)S(1)}, f32[1024,4,64]{0,2,1:T(8,128)}, f32[2,512,4,64]{1,3,2,0:T(8,128)}, s32[2]{0:T(128)S(1)}, /*inde...) while((s32[]{:T(128)}, f32[1024,4,64]{0,2,1:T(8,128)S(1)}, ...), condition=%wide.region_10.10_spmd.clone, body=%wide.region_8.9_spmd.clone.sunk | while | flops 1375598592 | bytes 89196952 | solution.py:198
  616.2 19.9 dynamic_update_slice.44
  636.1 19.9 dynamic_update_slice.45
  661.3 33.3 %while.47 = (s32[]{:T(128)}, f32[1024,4,64]{0,2,1:T(8,128)S(1)}, f32[1024,4,64]{0,2,1:T(8,128)}, f32[2,512,4,64]{1,3,2,0:T(8,128)}, s32[2]{0:T(128)S(1)}, /*inde...) while((s32[]{:T(128)}, f32[1024,4,64]{0,2,1:T(8,128)S(1)}, ...), condition=%wide.region_10.10_spmd.clone, body=%wide.region_8.9_spmd.clone.sunk | while | flops 1375598592 | bytes 89196952 | solution.py:198
  701.8 19.9 dynamic_update_slice.44
  721.7 19.9 dynamic_update_slice.45
  746.9 33.3 %while.47 = (s32[]{:T(128)}, f32[1024,4,64]{0,2,1:T(8,128)S(1)}, f32[1024,4,64]{0,2,1:T(8,128)}, f32[2,512,4,64]{1,3,2,0:T(8,128)}, s32[2]{0:T(128)S(1)}, /*inde...) while((s32[]{:T(128)}, f32[1024,4,64]{0,2,1:T(8,128)S(1)}, ...), condition=%wide.region_10.10_spmd.clone, body=%wide.region_8.9_spmd.clone.sunk | while | flops 1375598592 | bytes 89196952 | solution.py:198
  787.4 19.9 dynamic_update_slice.44
  807.3 19.9 dynamic_update_slice.45
  832.5 33.3 %while.47 = (s32[]{:T(128)}, f32[1024,4,64]{0,2,1:T(8,128)S(1)}, f32[1024,4,64]{0,2,1:T(8,128)}, f32[2,512,4,64]{1,3,2,0:T(8,128)}, s32[2]{0:T(128)S(1)}, /*inde...) while((s32[]{:T(128)}, f32[1024,4,64]{0,2,1:T(8,128)S(1)}, ...), condition=%wide.region_10.10_spmd.clone, body=%wide.region_8.9_spmd.clone.sunk | while | flops 1375598592 | bytes 89196952 | solution.py:198
  873.0 19.9 dynamic_update_slice.44
  892.9 19.9 dynamic_update_slice.45
  917.1 4.2 fusion.70
  929.1 13.1 fusion.81
  942.3 13.5 fusion.82
  959.7 13.1 fusion.83
  972.8 23.4 %fusion.80 = f32[4096,1024]{1,0:T(8,128)} fusion(bf16[4096,2048]{1,0:T(8,128)(2,1)} %all-gather.9.cloned.1.call-done, bf16[2048,1024]{1,0:T(8,128)(2,1)} %all-gather.19.cloned.1.call-done), kind=kOutput, calls=%fused_computation.136 | convolution fusion | flops 17179869184 | bytes 37748736 | tf_op jit(solution)/shard_map/dot_general | solution.py:91
  996.2 36.5 %convert_reduce_fusion = (f32[1024]{0:T(1024)}, bf16[4096,1024]{1,0:T(8,128)(2,1)}) fusion(f32[4096,1024]{1,0:T(8,128)} %fusion.80, f32[1024]{0:T(1024)S(1)} %copy-done.40, bf16[4096,2048]{1,0:T(8,128)(2,1)} %all-gather.23.cloned.1.call-done, bf16[1024,2048]{1,0:T(8,128)(2,1)} %all-gather.21.cloned.1.call-done), kind=kOutput, calls=%fused_computation.68 | convolution fusion | flops 17276338176 | bytes 46145536 | tf_op jit(solution)/shard_map/rd,fd->rf/dot_general | solution.py:151
  1032.6 48.6 %add_add_fusion = f32[4096,2048]{1,0:T(8,128)} fusion(f32[4096,2048]{1,0:T(8,128)} %fusion.83, f32[4096,2048]{1,0:T(8,128)} %fusion.81, f32[4096,2048]{1,0:T(8,128)} %fusion.82, bf16[4096,1024]{1,0:T(8,128)(2,1)} %get-tuple-element.433, bf16[2048,1024]{1,0:T(8,128)(2,1)} %all-gather.19.cloned.1.call-done), kind=kOutput, calls=%fused_computation.57 | convolution fusion | flops 17205035008 | bytes 146800640 | tf_op jit(solution)/shard_map/rf,df->rd/dot_general | solution.py:223
  1086.3 13.4 fusion.79
  1099.7 34.0 %convolution_add_fusion = f32[4096,2048]{1,0:T(8,128)} fusion(f32[4096,2048]{1,0:T(8,128)} %fusion.79, bf16[1024,2048]{1,0:T(8,128)(2,1)S(1)} %copy-done.42, f32[4096,1024]{1,0:T(8,128)} %fusion.80, f32[1024]{0:T(1024)S(1)} %copy-done.40), kind=kOutput, calls=%fused_computation.60 | convolution fusion | flops 17230200832 | bytes 88084480 | tf_op jit(solution)/shard_map/dot_general | solution.py:128
  1133.7 12.5 fusion.87
  1146.8 9.8 fusion.86
  1156.7 13.1 fusion.85
  1169.8 9.8 fusion.84
  1179.9 24.2 %fusion.88 = f32[2048,1024]{1,0:T(8,128)} fusion(bf16[4096,2048]{1,0:T(8,128)(2,1)} %all-gather.9.cloned.1.call-done, bf16[4096,1024]{1,0:T(8,128)(2,1)} %get-tuple-element.433), kind=kOutput, calls=%fused_computation.144 | convolution fusion | flops 17179869184 | bytes 33554432 | tf_op jit(solution)/shard_map/rd,rf->df/dot_general | solution.py:218
  1204.2 28.9 %fusion.76 = f32[1024,2048]{1,0:T(8,128)} fusion(bf16[4096,2048]{1,0:T(8,128)(2,1)} %all-gather.23.cloned.1.call-done, f32[4096,1024]{1,0:T(8,128)} %fusion.80, f32[1024]{0:T(1024)S(1)} %copy-done.40), kind=kOutput, calls=%fused_computation.133 | convolution fusion | flops 17221812224 | bytes 41947136 | tf_op jit(solution)/shard_map/rf,rd->fd/dot_general | solution.py:147
  1236.1 10.8 all-reduce.1
  1246.9 158.2 %reduce-scatter.11.cloned.1.call-done = f32[512,2048]{1,0:T(8,128)} async-done(((f32[4096,2048]{1,0:T(8,128)}), f32[512,2048]{1,0:T(8,128)}) %reduce-scatter.11.cloned.1.call-update) | async-done | bytes 4194320 | tf_op jit(solution)/shard_map/reduce_scatter | solution.py:219
  1410.6 320.8 %reduce-scatter.9.cloned.1.call-done = f32[512,2048]{1,0:T(8,128)} async-done(((f32[4096,2048]{1,0:T(8,128)}), f32[512,2048]{1,0:T(8,128)}) %reduce-scatter.9.cloned.1.call-update) | async-done | bytes 4194320 | tf_op jit(solution)/shard_map/reduce_scatter | solution.py:126
  1731.4 7.6 convert_reduce_fusion.2
  1739.0 38.3 %all-reduce = (f32[2048]{0:T(1024)}, f32[2048]{0:T(1024)}, f32[2048]{0:T(1024)S(1)}) all-reduce(f32[2048]{0:T(1024)S(1)} %get-tuple-element.359, f32[2048]{0:T(1024)S(1)} %get-tuple-element.361, f32[2048]{0:T(1024)S(1)} %get-tuple-element.458), channel_id=1, replica_groups=mesh['dp'=4,'tensor'=8] {'dp','tensor'}, use_global_device_ids=true, to_apply=%region_16.17 | all-reduce | flops 6144 | bytes 49152 | tf_op jit(solution)/shard_map/psum | solution.py:232
  1777.3 30.9 %reduce-scatter.17.cloned.1.call-done = f32[512,256]{1,0:T(8,128)} async-done(((f32[2048,256]{1,0:T(8,128)}), f32[512,256]{1,0:T(8,128)}) %reduce-scatter.17.cloned.1.call-update) | async-done | bytes 524304 | tf_op jit(solution)/shard_map/reduce_scatter | solution.py:254
  1808.2 38.7 %reduce-scatter.15.cloned.1.call-done = f32[512,256]{1,0:T(8,128)} async-done(((f32[2048,256]{1,0:T(8,128)}), f32[512,256]{1,0:T(8,128)}) %reduce-scatter.15.cloned.1.call-update) | async-done | bytes 524304 | tf_op jit(solution)/shard_map/reduce_scatter | solution.py:253
  1847.0 38.9 %reduce-scatter.13.cloned.1.call-done = f32[512,256]{1,0:T(8,128)} async-done(((f32[2048,256]{1,0:T(8,128)}), f32[512,256]{1,0:T(8,128)}) %reduce-scatter.13.cloned.1.call-update) | async-done | bytes 524304 | tf_op jit(solution)/shard_map/reduce_scatter | solution.py:252
  1885.9 89.9 %reduce-scatter.21.cloned.1.call-done = f32[512,1024]{1,0:T(8,128)} async-done(((f32[2048,1024]{1,0:T(8,128)}), f32[512,1024]{1,0:T(8,128)}) %reduce-scatter.21.cloned.1.call-update) | async-done | bytes 2097168 | tf_op jit(solution)/shard_map/reduce_scatter | solution.py:255
  1975.8 90.2 %reduce-scatter.23.cloned.1.call-done = f32[1024,512]{1,0:T(8,128)} async-done(((f32[1024,2048]{1,0:T(8,128)}), f32[1024,512]{1,0:T(8,128)}) %reduce-scatter.23.cloned.1.call-update) | async-done | bytes 2097168 | tf_op jit(solution)/shard_map/reduce_scatter | solution.py:257
  (428 shorter events, 266.9 us)
Async XLA Ops:
  7.2 7.6 copy-start.1
  7.2 32.0 %all-gather.15.cloned.1.call-start = ((), (), s32[]{:S(2)}) async-start(), calls=%async_computation.11 | async-start | bytes 1310720 | tf_op jit(solution)/shard_map/all_gather | solution.py:81
  7.9 184.6 %all-gather.9.cloned.1.call-start = ((), (), s32[]{:S(2)}) async-start(), calls=%async_computation.8 | async-start | bytes 18874368 | tf_op jit(solution)/shard_map/all_gather | solution.py:87
  8.7 5.5 copy-start.25
  11.3 2.9 copy-start.28
  16.9 4.1 copy-start.43
  16.9 4.1 copy-start.44
  16.9 4.2 copy-start.45
  16.9 4.2 copy-start.41
  17.0 205.3 %all-gather.13.cloned.1.call-start = ((), (), s32[]{:S(2)}) async-start(), calls=%async_computation.10 | async-start | bytes 1310720 | tf_op jit(solution)/shard_map/all_gather | solution.py:80
  17.7 234.8 %all-gather.11.cloned.1.call-start = ((), (), s32[]{:S(2)}) async-start(), calls=%async_computation.9 | async-start | bytes 1310720 | tf_op jit(solution)/shard_map/all_gather | solution.py:82
  18.3 260.3 %all-gather.17.cloned.1.call-start = ((), (), s32[]{:S(2)}) async-start(), calls=%async_computation.12 | async-start | bytes 1310720 | tf_op jit(solution)/shard_map/all_gather | solution.py:84
  18.9 409.6 %all-gather.23.cloned.1.call-start = ((), (), s32[]{:S(2)}) async-start(), calls=%async_computation.16 | async-start | bytes 18874368 | tf_op jit(solution)/shard_map/all_gather | solution.py:145
  19.4 953.3 %all-gather.19.cloned.1.call-start = ((), (), s32[]{:S(2)}) async-start(), calls=%async_computation.13 | async-start | bytes 5242880 | tf_op jit(solution)/shard_map/all_gather | solution.py:83
  20.2 976.0 %all-gather.21.cloned.1.call-start = ((), (), s32[]{:S(2)}) async-start(), calls=%async_computation.14 | async-start | bytes 5242880 | tf_op jit(solution)/shard_map/all_gather | solution.py:85
  20.9 1384.2 %reduce-scatter.11.cloned.1.call-start = ((), (), s32[]{:S(2)}) async-start(), calls=%async_computation.17 | async-start | bytes 37748736 | tf_op jit(solution)/shard_map/reduce_scatter | solution.py:219
  22.7 432.1 %copy-start.20 = (f32[1024,32]{0,1:T(8,128)}, f32[1024,32]{0,1:T(8,128)S(1)}, u32[]{:S(2)}) copy-start(f32[1024,32]{0,1:T(8,128)S(1)} %get-tuple-element.467) | copy-start | bytes 393220
  462.2 4.0 copy-start.17
  462.3 4.0 copy-start.27
  569.0 1.3 copy-start.18
  583.2 3.2 copy-start.7
  599.9 3.2 copy-start.7
  614.1 22.1 %copy-start = (f32[1,1024,4,64]{1,0,3,2:T(1,128)S(1)}, f32[1,1024,4,64]{1,0,3,2:T(1,128)}, u32[]{:S(2)}) copy-start(f32[1,1024,4,64]{1,0,3,2:T(1,128)} %copy.103) | copy-start | bytes 3145732 | tf_op jit(solution)/shard_map/while
  668.8 3.2 copy-start.7
  685.5 3.2 copy-start.7
  699.6 22.1 %copy-start = (f32[1,1024,4,64]{1,0,3,2:T(1,128)S(1)}, f32[1,1024,4,64]{1,0,3,2:T(1,128)}, u32[]{:S(2)}) copy-start(f32[1,1024,4,64]{1,0,3,2:T(1,128)} %copy.103) | copy-start | bytes 3145732 | tf_op jit(solution)/shard_map/while
  754.4 3.2 copy-start.7
  771.0 3.2 copy-start.7
  785.2 22.1 %copy-start = (f32[1,1024,4,64]{1,0,3,2:T(1,128)S(1)}, f32[1,1024,4,64]{1,0,3,2:T(1,128)}, u32[]{:S(2)}) copy-start(f32[1,1024,4,64]{1,0,3,2:T(1,128)} %copy.103) | copy-start | bytes 3145732 | tf_op jit(solution)/shard_map/while
  840.0 3.2 copy-start.7
  856.6 3.2 copy-start.7
  870.8 22.1 %copy-start = (f32[1,1024,4,64]{1,0,3,2:T(1,128)S(1)}, f32[1,1024,4,64]{1,0,3,2:T(1,128)}, u32[]{:S(2)}) copy-start(f32[1,1024,4,64]{1,0,3,2:T(1,128)} %copy.103) | copy-start | bytes 3145732 | tf_op jit(solution)/shard_map/while
  913.0 2.8 copy-start.15
  913.0 4.1 copy-start.16
  925.2 17.1 copy-start.10
  925.2 3.9 copy-start.23
  929.1 13.2 copy-start.8
  929.1 13.2 copy-start.21
  942.3 13.6 copy-start.14
  955.8 3.9 copy-start.24
  958.3 1.3 copy-start.11
  972.8 23.4 %copy-start.40 = (f32[1024]{0:T(1024)S(1)}, f32[1024]{0:T(1024)}, u32[]{:S(2)}) copy-start(f32[1024]{0:T(1024)} %convert_element_type.123) | copy-start | bytes 12292
  1081.3 1.6 copy-start.19
  1081.3 650.1 %reduce-scatter.9.cloned.1.call-start = ((), (), s32[]{:S(2)}) async-start(), calls=%async_computation.15 | async-start | bytes 37748736 | tf_op jit(solution)/shard_map/reduce_scatter | solution.py:126
  1082.9 3.4 copy-start.22
  1086.3 13.4 copy-start.42
  1133.7 13.1 copy-start.12
  1133.7 643.6 %reduce-scatter.19.cloned.1.call-start = ((), (), s32[]{:S(2)}) async-start(), calls=%async_computation.21 | async-start | bytes 2621440 | tf_op jit(solution)/shard_map/reduce_scatter | solution.py:256
  1146.3 661.9 %reduce-scatter.17.cloned.1.call-start = ((), (), s32[]{:S(2)}) async-start(), calls=%async_computation.20 | async-start | bytes 2621440 | tf_op jit(solution)/shard_map/reduce_scatter | solution.py:254
  1156.6 13.2 copy-start.9
  1156.6 690.4 %reduce-scatter.15.cloned.1.call-start = ((), (), s32[]{:S(2)}) async-start(), calls=%async_computation.19 | async-start | bytes 2621440 | tf_op jit(solution)/shard_map/reduce_scatter | solution.py:253
  1169.7 716.2 %reduce-scatter.13.cloned.1.call-start = ((), (), s32[]{:S(2)}) async-start(), calls=%async_computation.18 | async-start | bytes 2621440 | tf_op jit(solution)/shard_map/reduce_scatter | solution.py:252
  1179.7 796.2 %reduce-scatter.21.cloned.1.call-start = ((), (), s32[]{:S(2)}) async-start(), calls=%async_computation.22 | async-start | bytes 10485760 | tf_op jit(solution)/shard_map/reduce_scatter | solution.py:255
  1204.2 861.9 %reduce-scatter.23.cloned.1.call-start = ((), (), s32[]{:S(2)}) async-start(), calls=%async_computation.23 | async-start | bytes 10485760 | tf_op jit(solution)/shard_map/reduce_scatter | solution.py:257
  1233.1 2.9 copy-start.34
  1233.1 2.9 copy-start.35
  1233.1 3.0 copy-start.39
  1233.1 172.1 %copy-start.2 = (bf16[512,2048]{1,0:T(8,128)(2,1)S(1)}, bf16[512,2048]{1,0:T(8,128)(2,1)}, u32[]{:S(2)}) copy-start(bf16[512,2048]{1,0:T(8,128)(2,1)} %param.23) | copy-start | bytes 6291460
  1233.1 172.0 %copy-start.26 = (f32[2048]{0:T(1024)S(1)}, f32[2048]{0:T(1024)}, u32[]{:S(2)}) copy-start(f32[2048]{0:T(1024)} %copy-done.25) | copy-start | bytes 24580
  1233.1 172.0 %copy-start.29 = (f32[512]{0:T(512)S(1)}, f32[512]{0:T(512)}, u32[]{:S(2)}) copy-start(f32[512]{0:T(512)} %copy-done.28) | copy-start | bytes 6148
  1233.8 174.7 %copy-start.33 = (f32[512]{0:T(512)S(1)}, f32[512]{0:T(512)}, u32[]{:S(2)}) copy-start(f32[512]{0:T(512)} %copy-done.32) | copy-start | bytes 6148
  1233.8 174.7 %copy-start.31 = (f32[512]{0:T(512)S(1)}, f32[512]{0:T(512)}, u32[]{:S(2)}) copy-start(f32[512]{0:T(512)} %copy-done.30) | copy-start | bytes 6148
  1405.1 3.5 copy-start.3
  1777.3 289.3 %copy-start.36 = (f32[2048]{0:T(1024)}, f32[2048]{0:T(1024)S(1)}, u32[]{:S(2)}) copy-start(f32[2048]{0:T(1024)S(1)} %get-tuple-element.893) | copy-start | bytes 24580
  (29 other events, 32.0 us)
Sparse Core Ops, SparseCore 0:
  9.9 29.3 all-gather.14
  41.4 151.0 all-gather.8
  194.4 24.8 all-gather.12
  221.0 26.6 all-gather.10
  249.3 26.4 all-gather.16
  277.3 151.1 all-gather.22
  430.3 50.9 all-gather.18
  483.1 52.5 all-gather.20
  1081.4 323.6 reduce-scatter.10
  1407.5 323.8 reduce-scatter.8
  1735.0 34.3 reduce-scatter.18
  1773.0 35.1 reduce-scatter.16
  1811.8 35.1 reduce-scatter.14
  1850.7 35.2 reduce-scatter.12
  1889.4 86.3 reduce-scatter.20
  1979.6 86.3 reduce-scatter.22
where the time goes:
time: 2090 us; the launch traced here: 2070 us
  waiting for transfers between devices  1090 us (52%)
  matrix products  473 us (23%)
  local copies, waits for them, and re-layouts  297 us (14%)
  other arithmetic  95.4 us (5%)
  loops' own time  51.3 us (2%)
  blocking collectives  49.1 us (2%)
    reduce_scatter x1, waiting for transfers between devices, per_device(): lax.psum_scatter(jnp.dot(attended_low, full_out, preferred_element_type=j...  321 us
    dynamic_update_slice x20, local copies, waits for them, and re-layouts, per_device(): lax.map(backward_sequence, jnp.arange(seq_count))  181 us
    reduce_scatter x1, waiting for transfers between devices, per_device(): lax.psum_scatter(jnp.einsum('rk,dk->rd', query_grad, back_query, preferre...  158 us
    all_gather x1, waiting for transfers between devices, per_device(): group_rows = lax.all_gather(normed, 'tensor', axis=0, tiled=True)  153 us
    all_gather x1, waiting for transfers between devices, per_device(): upstream = lax.all_gather(grad_out, 'tensor', axis=0, tiled=True)  150 us
    reduce_scatter x1, waiting for transfers between devices, per_device(): lax.psum_scatter(down_wgrad, 'dp', scatter_dimension=1, tiled=True)  90.2 us
    reduce_scatter x1, waiting for transfers between devices, per_device(): lax.psum_scatter(up_wgrad, 'dp', scatter_dimension=0, tiled=True)  89.9 us
    dot_general x4, matrix products, project(): jnp.dot(group_rows, weight_part, preferred_element_type=jnp.float32)  60.7 us
  transfers between devices with their start and end apart: 16, of which 10 were waited for; matrix products, arithmetic and copies ran while one was open for 37% of the time, Pallas kernels for 0%

commit v1 on v0

--- a/solution.py
+++ b/solution.py
@@ -84,7 +84,14 @@
         lax.all_gather(out_weight, "dp", axis=1, tiled=True),
         lax.all_gather(down_weight, "dp", axis=1, tiled=True),
     )
-    group_rows = lax.all_gather(normed, "tensor", axis=0, tiled=True)
+    ring = [normed]
+    for hop in range(7):
+        ring.append(lax.ppermute(ring[-1], "tensor", [(dev, (dev + 1) % 8) for dev in range(8)]))
+    group_rows = jnp.roll(
+        jnp.concatenate(ring[::-1], axis=0),
+        (lax.axis_index("tensor") + 1) * ring[0].shape[0],
+        axis=0,
+    )
     cos_table, sin_table = rotary_tables(length, ROT)
 
     def project(weight_part, bias_part):

time: 2090 us -> 2020 us (0.967)
  waiting for transfers between devices: 1090 us -> 995 us
  local copies, waits for them, and re-layouts: 297 us -> 333 us
    ppermute x0 -> x7, waiting for transfers between devices: none -> 225 us  [per_device(): lax.ppermute(ring[-1], 'tensor', [(dev, (dev + 1) % 8) for dev in range(8)])]
    all_gather x1, waiting for transfers between devices: 153 us -> 0.02 us  [per_device(): back_rows = lax.all_gather(normed, 'tensor', axis=0, tiled=True)]
    all_gather x1, waiting for transfers between devices: 150 us -> 0.01 us  [per_device(): upstream = lax.all_gather(grad_out, 'tensor', axis=0, tiled=True)]
    unnamed x87 -> x119, local copies, waits for them, and re-layouts: 12.6 us -> 49.5 us
    reduce_scatter x1, waiting for transfers between devices: 30.9 us -> 0.02 us  [per_device(): lax.psum_scatter(value_wgrad, 'dp', scatter_dimension=0, tiled=True)]
    reduce_scatter x1, waiting for transfers between devices: 0.02 us -> 30.9 us  [per_device(): lax.psum_scatter(out_wgrad, 'dp', scatter_dimension=1, tiled=True)]
  transfers between devices with their start and end apart: 16 -> 23, of which waited for: 10 -> 14; matrix products, arithmetic and copies ran while one was open for 37% -> 44% of each run, Pallas kernels for 0% -> 0%
where the time goes in v1:
time: 2020 us; the launch traced here: 2010 us
  waiting for transfers between devices  995 us (49%)
  matrix products  472 us (23%)
  local copies, waits for them, and re-layouts  333 us (16%)
  other arithmetic  91.9 us (5%)
  loops' own time  51.6 us (3%)
  blocking collectives  50.7 us (3%)
    reduce_scatter x1, waiting for transfers between devices, per_device(): lax.psum_scatter(jnp.dot(attended_low, full_out, preferred_element_type=j...  321 us
    ppermute x7, waiting for transfers between devices, per_device(): lax.ppermute(ring[-1], 'tensor', [(dev, (dev + 1) % 8) for dev in range(8)])  225 us
    dynamic_update_slice x20, local copies, waits for them, and re-layouts, per_device(): lax.map(backward_sequence, jnp.arange(seq_count))  181 us
    reduce_scatter x1, waiting for transfers between devices, per_device(): lax.psum_scatter(jnp.einsum('rk,dk->rd', query_grad, back_query, preferre...  157 us
    reduce_scatter x1, waiting for transfers between devices, per_device(): lax.psum_scatter(down_wgrad, 'dp', scatter_dimension=1, tiled=True)  90.2 us
    reduce_scatter x1, waiting for transfers between devices, per_device(): lax.psum_scatter(up_wgrad, 'dp', scatter_dimension=0, tiled=True)  89.9 us
    dot_general x4, matrix products, project(): jnp.dot(group_rows, weight_part, preferred_element_type=jnp.float32)  61.5 us
    unnamed x119, local copies, waits for them, and re-layouts  49.5 us
  transfers between devices with their start and end apart: 23, of which 14 were waited for; matrix products, arithmetic and copies ran while one was open for 44% of the time, Pallas kernels for 0%

profile of v1, /device:TPU:0, one launch (start us, length us, event | category | flops | bytes accessed | tf_op | source)
XLA Modules:
  0.0 2011.1 jit_solution(7647000457288992646)
XLA Ops:
  15.0 28.0 %collective-permute-done = bf16[512,2048]{1,0:T(8,128)(2,1)S(1)} collective-permute-done((bf16[512,2048]{1,0:T(8,128)(2,1)}, bf16[512,2048]{1,0:T(8,128)(2,1)S(1)}, u32[]{:S(2)}, u32[]{:S(2)}) %collective-permute-start) | collective-permute-done | bytes 2097184 | tf_op jit(solution)/shard_map/ppermute | solution.py:89
  44.4 27.3 %collective-permute-done.1 = bf16[512,2048]{1,0:T(8,128)(2,1)S(1)} collective-permute-done((bf16[512,2048]{1,0:T(8,128)(2,1)S(1)}, bf16[512,2048]{1,0:T(8,128)(2,1)S(1)}, u32[]{:S(2)}, u32[]{:S(2)}) %collective-permute-start.1) | collective-permute-done | bytes 2097184 | tf_op jit(solution)/shard_map/ppermute | solution.py:89
  72.9 27.4 %collective-permute-done.2 = bf16[512,2048]{1,0:T(8,128)(2,1)} collective-permute-done((bf16[512,2048]{1,0:T(8,128)(2,1)S(1)}, bf16[512,2048]{1,0:T(8,128)(2,1)}, u32[]{:S(2)}, u32[]{:S(2)}) %collective-permute-start.2) | collective-permute-done | bytes 2097184 | tf_op jit(solution)/shard_map/ppermute | solution.py:89
  100.4 27.5 %collective-permute-done.3 = bf16[512,2048]{1,0:T(8,128)(2,1)} collective-permute-done((bf16[512,2048]{1,0:T(8,128)(2,1)}, bf16[512,2048]{1,0:T(8,128)(2,1)}, u32[]{:S(2)}, u32[]{:S(2)}) %collective-permute-start.3) | collective-permute-done | bytes 2097184 | tf_op jit(solution)/shard_map/ppermute | solution.py:89
  127.9 27.5 %collective-permute-done.4 = bf16[512,2048]{1,0:T(8,128)(2,1)S(1)} collective-permute-done((bf16[512,2048]{1,0:T(8,128)(2,1)}, bf16[512,2048]{1,0:T(8,128)(2,1)S(1)}, u32[]{:S(2)}, u32[]{:S(2)}) %collective-permute-start.4) | collective-permute-done | bytes 2097184 | tf_op jit(solution)/shard_map/ppermute | solution.py:89
  156.7 27.4 %collective-permute-done.5 = bf16[512,2048]{1,0:T(8,128)(2,1)} collective-permute-done((bf16[512,2048]{1,0:T(8,128)(2,1)S(1)}, bf16[512,2048]{1,0:T(8,128)(2,1)}, u32[]{:S(2)}, u32[]{:S(2)}) %collective-permute-start.5) | collective-permute-done | bytes 2097184 | tf_op jit(solution)/shard_map/ppermute | solution.py:89
  186.1 59.8 %collective-permute-done.6 = bf16[512,2048]{1,0:T(8,128)(2,1)} collective-permute-done((bf16[512,2048]{1,0:T(8,128)(2,1)}, bf16[512,2048]{1,0:T(8,128)(2,1)}, u32[]{:S(2)}, u32[]{:S(2)}) %collective-permute-start.6) | collective-permute-done | bytes 2097184 | tf_op jit(solution)/shard_map/ppermute | solution.py:89
  285.1 12.7 fusion.64
  297.8 5.9 copy.53
  303.7 6.0 reshape.271
  315.0 12.6 fusion.67
  327.7 5.7 copy.54
  333.3 6.6 reshape.272
  345.6 12.0 fusion.70
  357.6 7.2 reshape.277
  364.7 6.9 copy.55
  371.6 4.0 fusion.85
  382.4 103.1 %while.44 = (s32[]{:T(128)}, bf16[8,512,4,64]{1,3,2,0:T(8,128)(2,1)S(1)}, f32[8,4,512]{2,1,0:T(4,128)S(1)}, s32[8]{0:T(128)S(1)}, bf16[4,1024,4,64]{1,3,2,0:T(8,...) while((s32[]{:T(128)}, ...), condition=%wide.region_5.6_spmd, body=%wide.region_2.5_spmd.sunk | while | flops 562558976 | bytes 29182452 | solution.py:129
  391.7 3.6 fusion.166
  404.5 3.6 fusion.166
  417.5 3.6 fusion.166
  430.4 3.7 fusion.166
  443.2 3.7 fusion.166
  456.1 3.7 fusion.166
  468.9 3.7 fusion.166
  485.5 24.2 %fusion.49 = f32[4096,1024]{1,0:T(8,128)} fusion(bf16[2048,1024]{1,0:T(8,128)(2,1)} %all-gather.17.cloned.1.call-done, bf16[8192,2048]{1,0:T(8,128)(2,1)} %constant_dynamic-update-slice_fusion, s32[]{:T(128)S(6)} %select_n.83), kind=kOutput, calls=%fused_computation.70 | convolution fusion | flops 17179869184 | bytes 37748740 | tf_op jit(solution)/shard_map/dot_general | solution.py:98
  509.7 10.7 convolution_convert_fusion
  523.7 7.0 copy.63
  530.8 343.6 %while.46 = (s32[]{:T(128)}, f32[4,1024,4,64]{1,0,3,2:T(4,128)}, f32[4,1024,4,64]{1,0,3,2:T(4,128)}, bf16[4,1024,4,64]{1,3,2,0:T(8,128)(2,1)}, s32[4]{0:T(128)S(...) while((s32[]{:T(128)}, f32[4,1024,4,64]{1,0,3,2:T(4,128)}, ...), condition=%wide.region_11.12_spmd, body=%wide.region_7.11_spmd.sunk | while | flops 1375598592 | bytes 110209856 | solution.py:210
  536.4 33.4 %while.47 = (s32[]{:T(128)}, f32[1024,4,64]{0,2,1:T(8,128)S(1)}, f32[1024,4,64]{0,2,1:T(8,128)}, f32[2,512,4,64]{1,3,2,0:T(8,128)}, s32[2]{0:T(128)S(1)}, /*inde...) while((s32[]{:T(128)}, f32[1024,4,64]{0,2,1:T(8,128)S(1)}, ...), condition=%wide.region_10.10_spmd.clone, body=%wide.region_8.9_spmd.clone.sunk | while | flops 1375598592 | bytes 89196952 | solution.py:205
  577.1 19.9 dynamic_update_slice.44
  597.0 20.0 dynamic_update_slice.45
  622.2 33.4 %while.47 = (s32[]{:T(128)}, f32[1024,4,64]{0,2,1:T(8,128)S(1)}, f32[1024,4,64]{0,2,1:T(8,128)}, f32[2,512,4,64]{1,3,2,0:T(8,128)}, s32[2]{0:T(128)S(1)}, /*inde...) while((s32[]{:T(128)}, f32[1024,4,64]{0,2,1:T(8,128)S(1)}, ...), condition=%wide.region_10.10_spmd.clone, body=%wide.region_8.9_spmd.clone.sunk | while | flops 1375598592 | bytes 89196952 | solution.py:205
  662.8 19.9 dynamic_update_slice.44
  682.8 20.0 dynamic_update_slice.45
  707.9 33.4 %while.47 = (s32[]{:T(128)}, f32[1024,4,64]{0,2,1:T(8,128)S(1)}, f32[1024,4,64]{0,2,1:T(8,128)}, f32[2,512,4,64]{1,3,2,0:T(8,128)}, s32[2]{0:T(128)S(1)}, /*inde...) while((s32[]{:T(128)}, f32[1024,4,64]{0,2,1:T(8,128)S(1)}, ...), condition=%wide.region_10.10_spmd.clone, body=%wide.region_8.9_spmd.clone.sunk | while | flops 1375598592 | bytes 89196952 | solution.py:205
  748.6 19.9 dynamic_update_slice.44
  768.5 20.0 dynamic_update_slice.45
  793.7 33.4 %while.47 = (s32[]{:T(128)}, f32[1024,4,64]{0,2,1:T(8,128)S(1)}, f32[1024,4,64]{0,2,1:T(8,128)}, f32[2,512,4,64]{1,3,2,0:T(8,128)}, s32[2]{0:T(128)S(1)}, /*inde...) while((s32[]{:T(128)}, f32[1024,4,64]{0,2,1:T(8,128)S(1)}, ...), condition=%wide.region_10.10_spmd.clone, body=%wide.region_8.9_spmd.clone.sunk | while | flops 1375598592 | bytes 89196952 | solution.py:205
  834.4 19.9 dynamic_update_slice.44
  854.3 20.0 dynamic_update_slice.45
  892.6 13.1 fusion.103
  905.7 13.6 fusion.104
  919.3 13.1 fusion.105
  932.4 36.3 %convert_reduce_fusion = (f32[1024]{0:T(1024)}, bf16[4096,1024]{1,0:T(8,128)(2,1)}) fusion(f32[4096,1024]{1,0:T(8,128)} %fusion.49, f32[1024]{0:T(1024)S(1)} %copy-done.49, bf16[4096,2048]{1,0:T(8,128)(2,1)} %all-gather.21.cloned.1.call-done, bf16[1024,2048]{1,0:T(8,128)(2,1)} %all-gather.19.cloned.1.call-done), kind=kOutput, calls=%fused_computation.68 | convolution fusion | flops 17276338176 | bytes 46145536 | tf_op jit(solution)/shard_map/rd,fd->rf/dot_general | solution.py:158
  968.7 48.6 %add_add_fusion = f32[4096,2048]{1,0:T(8,128)} fusion(f32[4096,2048]{1,0:T(8,128)} %fusion.105, f32[4096,2048]{1,0:T(8,128)} %fusion.103, f32[4096,2048]{1,0:T(8,128)} %fusion.104, bf16[4096,1024]{1,0:T(8,128)(2,1)} %get-tuple-element.433, bf16[2048,1024]{1,0:T(8,128)(2,1)} %all-gather.17.cloned.1.call-done), kind=kOutput, calls=%fused_computation.57 | convolution fusion | flops 17205035008 | bytes 146800640 | tf_op jit(solution)/shard_map/rf,df->rd/dot_general | solution.py:230
  1022.3 13.4 fusion.102
  1035.7 34.1 %convolution_add_fusion = f32[4096,2048]{1,0:T(8,128)} fusion(f32[4096,2048]{1,0:T(8,128)} %fusion.102, bf16[1024,2048]{1,0:T(8,128)(2,1)S(1)} %copy-done.51, f32[4096,1024]{1,0:T(8,128)} %fusion.49, f32[1024]{0:T(1024)S(1)} %copy-done.49), kind=kOutput, calls=%fused_computation.60 | convolution fusion | flops 17230200832 | bytes 88084480 | tf_op jit(solution)/shard_map/dot_general | solution.py:135
  1071.4 9.8 fusion.108
  1081.5 12.4 fusion.109
  1094.0 13.1 fusion.107
  1107.2 9.8 fusion.106
  1117.3 24.2 %fusion.110 = f32[2048,1024]{1,0:T(8,128)} fusion(bf16[4096,2048]{1,0:T(8,128)(2,1)} %all-gather.23.cloned.1.call-done, bf16[4096,1024]{1,0:T(8,128)(2,1)} %get-tuple-element.433), kind=kOutput, calls=%fused_computation.171 | convolution fusion | flops 17179869184 | bytes 33554432 | tf_op jit(solution)/shard_map/rd,rf->df/dot_general | solution.py:225
  1141.6 28.8 %fusion.99 = f32[1024,2048]{1,0:T(8,128)} fusion(bf16[4096,2048]{1,0:T(8,128)(2,1)} %all-gather.21.cloned.1.call-done, f32[4096,1024]{1,0:T(8,128)} %fusion.49, f32[1024]{0:T(1024)S(1)} %copy-done.49), kind=kOutput, calls=%fused_computation.161 | convolution fusion | flops 17221812224 | bytes 41947136 | tf_op jit(solution)/shard_map/rf,rd->fd/dot_general | solution.py:154
  1173.5 12.3 all-reduce.1
  1185.8 156.8 %reduce-scatter.11.cloned.1.call-done = f32[512,2048]{1,0:T(8,128)} async-done(((f32[4096,2048]{1,0:T(8,128)}), f32[512,2048]{1,0:T(8,128)}) %reduce-scatter.11.cloned.1.call-update) | async-done | bytes 4194320 | tf_op jit(solution)/shard_map/reduce_scatter | solution.py:226
  1348.1 320.8 %reduce-scatter.9.cloned.1.call-done = f32[512,2048]{1,0:T(8,128)} async-done(((f32[4096,2048]{1,0:T(8,128)}), f32[512,2048]{1,0:T(8,128)}) %reduce-scatter.9.cloned.1.call-update) | async-done | bytes 4194320 | tf_op jit(solution)/shard_map/reduce_scatter | solution.py:133
  1668.9 7.5 convert_reduce_fusion.2
  1676.4 38.4 %all-reduce = (f32[2048]{0:T(1024)}, f32[2048]{0:T(1024)}, f32[2048]{0:T(1024)S(1)}) all-reduce(f32[2048]{0:T(1024)S(1)} %get-tuple-element.359, f32[2048]{0:T(1024)S(1)} %get-tuple-element.361, f32[2048]{0:T(1024)S(1)} %get-tuple-element.458), channel_id=1, replica_groups=mesh['dp'=4,'tensor'=8] {'dp','tensor'}, use_global_device_ids=true, to_apply=%region_16.17 | all-reduce | flops 6144 | bytes 49152 | tf_op jit(solution)/shard_map/psum | solution.py:239
  1714.8 30.9 %reduce-scatter.19.cloned.1.call-done = f32[256,512]{1,0:T(8,128)} async-done(((f32[256,2048]{1,0:T(8,128)}), f32[256,512]{1,0:T(8,128)}) %reduce-scatter.19.cloned.1.call-update) | async-done | bytes 524304 | tf_op jit(solution)/shard_map/reduce_scatter | solution.py:263
  1745.7 38.8 %reduce-scatter.15.cloned.1.call-done = f32[512,256]{1,0:T(8,128)} async-done(((f32[2048,256]{1,0:T(8,128)}), f32[512,256]{1,0:T(8,128)}) %reduce-scatter.15.cloned.1.call-update) | async-done | bytes 524304 | tf_op jit(solution)/shard_map/reduce_scatter | solution.py:260
  1784.4 38.9 %reduce-scatter.13.cloned.1.call-done = f32[512,256]{1,0:T(8,128)} async-done(((f32[2048,256]{1,0:T(8,128)}), f32[512,256]{1,0:T(8,128)}) %reduce-scatter.13.cloned.1.call-update) | async-done | bytes 524304 | tf_op jit(solution)/shard_map/reduce_scatter | solution.py:259
  1823.3 89.9 %reduce-scatter.21.cloned.1.call-done = f32[512,1024]{1,0:T(8,128)} async-done(((f32[2048,1024]{1,0:T(8,128)}), f32[512,1024]{1,0:T(8,128)}) %reduce-scatter.21.cloned.1.call-update) | async-done | bytes 2097168 | tf_op jit(solution)/shard_map/reduce_scatter | solution.py:262
  1913.3 90.2 %reduce-scatter.23.cloned.1.call-done = f32[1024,512]{1,0:T(8,128)} async-done(((f32[1024,2048]{1,0:T(8,128)}), f32[1024,512]{1,0:T(8,128)}) %reduce-scatter.23.cloned.1.call-update) | async-done | bytes 2097168 | tf_op jit(solution)/shard_map/reduce_scatter | solution.py:264
  (476 shorter events, 318.2 us)
Async XLA Ops:
  7.2 4.0 copy-start.44
  7.2 4.0 copy-start.45
  7.2 4.1 copy-start
  7.2 277.9 %all-gather.11.cloned.1.call-start = ((), (), s32[]{:S(2)}) async-start(), calls=%async_computation.9 | async-start | bytes 1310720 | tf_op jit(solution)/shard_map/all_gather | solution.py:80
  7.9 307.1 %all-gather.13.cloned.1.call-start = ((), (), s32[]{:S(2)}) async-start(), calls=%async_computation.10 | async-start | bytes 1310720 | tf_op jit(solution)/shard_map/all_gather | solution.py:81
  8.7 336.9 %all-gather.9.cloned.1.call-start = ((), (), s32[]{:S(2)}) async-start(), calls=%async_computation.8 | async-start | bytes 1310720 | tf_op jit(solution)/shard_map/all_gather | solution.py:82
  9.4 476.1 %all-gather.17.cloned.1.call-start = ((), (), s32[]{:S(2)}) async-start(), calls=%async_computation.12 | async-start | bytes 5242880 | tf_op jit(solution)/shard_map/all_gather | solution.py:83
  10.0 499.7 %all-gather.15.cloned.1.call-start = ((), (), s32[]{:S(2)}) async-start(), calls=%async_computation.11 | async-start | bytes 1310720 | tf_op jit(solution)/shard_map/all_gather | solution.py:84
  10.6 499.1 %all-gather.21.cloned.1.call-start = ((), (), s32[]{:S(2)}) async-start(), calls=%async_computation.15 | async-start | bytes 18874368 | tf_op jit(solution)/shard_map/all_gather | solution.py:152
  11.2 921.2 %all-gather.19.cloned.1.call-start = ((), (), s32[]{:S(2)}) async-start(), calls=%async_computation.13 | async-start | bytes 5242880 | tf_op jit(solution)/shard_map/all_gather | solution.py:85
  11.2 271.7 %copy-start.32 = (f32[2048]{0:T(1024)}, f32[2048]{0:T(1024)S(1)}, u32[]{:S(2)}) copy-start(f32[2048]{0:T(1024)S(1)} %convert_element_type.113) | copy-start | bytes 24580
  11.6 271.3 %copy-start.35 = (f32[512]{0:T(512)}, f32[512]{0:T(512)S(1)}, u32[]{:S(2)}) copy-start(f32[512]{0:T(512)S(1)} %broadcast_multiply_fusion) | copy-start | bytes 6148
  12.3 172.7 %copy-start.39 = (f32[512]{0:T(512)}, f32[512]{0:T(512)S(1)}, u32[]{:S(2)}) copy-start(f32[512]{0:T(512)S(1)} %fusion.79) | copy-start | bytes 6148
  12.3 172.1 %copy-start.52 = (bf16[256]{0:T(256)(128)(2,1)S(1)}, bf16[256]{0:T(256)(128)(2,1)}, u32[]{:S(2)}) copy-start(bf16[256]{0:T(256)(128)(2,1)} %param.28) | copy-start | bytes 1540
  12.4 172.1 %copy-start.53 = (bf16[256]{0:T(256)(128)(2,1)S(1)}, bf16[256]{0:T(256)(128)(2,1)}, u32[]{:S(2)}) copy-start(bf16[256]{0:T(256)(128)(2,1)} %param.30) | copy-start | bytes 1540
  12.4 172.1 %copy-start.54 = (bf16[256]{0:T(256)(128)(2,1)S(1)}, bf16[256]{0:T(256)(128)(2,1)}, u32[]{:S(2)}) copy-start(bf16[256]{0:T(256)(128)(2,1)} %param.32) | copy-start | bytes 1540
  12.4 172.1 %copy-start.50 = (bf16[1024]{0:T(1024)(128)(2,1)S(1)}, bf16[1024]{0:T(1024)(128)(2,1)}, u32[]{:S(2)}) copy-start(bf16[1024]{0:T(1024)(128)(2,1)} %param.36) | copy-start | bytes 6148
  12.4 270.6 %copy-start.37 = (f32[512]{0:T(512)}, f32[512]{0:T(512)S(1)}, u32[]{:S(2)}) copy-start(f32[512]{0:T(512)S(1)} %fusion.93) | copy-start | bytes 6148
  14.6 28.4 %collective-permute-start = (bf16[512,2048]{1,0:T(8,128)(2,1)}, bf16[512,2048]{1,0:T(8,128)(2,1)S(1)}, u32[]{:S(2)}, u32[]{:S(2)}) collective-permute-start(bf16[512,2048]{1,0:T(8,128)(2,1)} %fusion.76), channel_id=1, source_target_pairs={{0,1},{1,2},{2,3},{3,4},{4,5},{5,6},{6,7},{7,0},{8,9},{9,10},{10,1... | collective-permute-start | bytes 6291464 | tf_op jit(solution)/shard_map/ppermute | solution.py:89
  44.4 27.3 %collective-permute-start.1 = (bf16[512,2048]{1,0:T(8,128)(2,1)S(1)}, bf16[512,2048]{1,0:T(8,128)(2,1)S(1)}, u32[]{:S(2)}, u32[]{:S(2)}) collective-permute-start(bf16[512,2048]{1,0:T(8,128)(2,1)S(1)} %collective-permute-done), channel_id=1, source_target_pairs={{0,1},{1,2},{2,3},{3,4},{4,5},{5,6},{6,7},{7,0},{8,9},{9,10},{10,1... | collective-permute-start | bytes 6291464 | tf_op jit(solution)/shard_map/ppermute | solution.py:89
  72.9 27.4 %collective-permute-start.2 = (bf16[512,2048]{1,0:T(8,128)(2,1)S(1)}, bf16[512,2048]{1,0:T(8,128)(2,1)}, u32[]{:S(2)}, u32[]{:S(2)}) collective-permute-start(bf16[512,2048]{1,0:T(8,128)(2,1)S(1)} %collective-permute-done.1), channel_id=1, source_target_pairs={{0,1},{1,2},{2,3},{3,4},{4,5},{5,6},{6,7},{7,0},{8,9},{9,10},{10,1... | collective-permute-start | bytes 6291464 | tf_op jit(solution)/shard_map/ppermute | solution.py:89
  100.3 27.6 %collective-permute-start.3 = (bf16[512,2048]{1,0:T(8,128)(2,1)}, bf16[512,2048]{1,0:T(8,128)(2,1)}, u32[]{:S(2)}, u32[]{:S(2)}) collective-permute-start(bf16[512,2048]{1,0:T(8,128)(2,1)} %collective-permute-done.2), channel_id=1, source_target_pairs={{0,1},{1,2},{2,3},{3,4},{4,5},{5,6},{6,7},{7,0},{8,9},{9,10},{10,1... | collective-permute-start | bytes 6291464 | tf_op jit(solution)/shard_map/ppermute | solution.py:89
  100.3 969.6 %all-gather.23.cloned.1.call-start = ((), (), s32[]{:S(2)}) async-start(), calls=%async_computation.17 | async-start | bytes 18874368 | tf_op jit(solution)/shard_map/all_gather | solution.py:151
  127.9 27.5 %collective-permute-start.4 = (bf16[512,2048]{1,0:T(8,128)(2,1)}, bf16[512,2048]{1,0:T(8,128)(2,1)S(1)}, u32[]{:S(2)}, u32[]{:S(2)}) collective-permute-start(bf16[512,2048]{1,0:T(8,128)(2,1)} %collective-permute-done.3), channel_id=1, source_target_pairs={{0,1},{1,2},{2,3},{3,4},{4,5},{5,6},{6,7},{7,0},{8,9},{9,10},{10,1... | collective-permute-start | bytes 6291464 | tf_op jit(solution)/shard_map/ppermute | solution.py:89
  156.7 27.4 %collective-permute-start.5 = (bf16[512,2048]{1,0:T(8,128)(2,1)S(1)}, bf16[512,2048]{1,0:T(8,128)(2,1)}, u32[]{:S(2)}, u32[]{:S(2)}) collective-permute-start(bf16[512,2048]{1,0:T(8,128)(2,1)S(1)} %collective-permute-done.4), channel_id=1, source_target_pairs={{0,1},{1,2},{2,3},{3,4},{4,5},{5,6},{6,7},{7,0},{8,9},{9,10},{10,1... | collective-permute-start | bytes 6291464 | tf_op jit(solution)/shard_map/ppermute | solution.py:89
  184.0 61.8 %collective-permute-start.6 = (bf16[512,2048]{1,0:T(8,128)(2,1)}, bf16[512,2048]{1,0:T(8,128)(2,1)}, u32[]{:S(2)}, u32[]{:S(2)}) collective-permute-start(bf16[512,2048]{1,0:T(8,128)(2,1)} %collective-permute-done.5), channel_id=1, source_target_pairs={{0,1},{1,2},{2,3},{3,4},{4,5},{5,6},{6,7},{7,0},{8,9},{9,10},{10,1... | collective-permute-start | bytes 6291464 | tf_op jit(solution)/shard_map/ppermute | solution.py:89
  184.1 1158.6 %reduce-scatter.11.cloned.1.call-start = ((), (), s32[]{:S(2)}) async-start(), calls=%async_computation.16 | async-start | bytes 37748736 | tf_op jit(solution)/shard_map/reduce_scatter | solution.py:226
  186.1 185.6 %copy-start.25 = (f32[1024,32]{0,1:T(8,128)}, f32[1024,32]{0,1:T(8,128)S(1)}, u32[]{:S(2)}) copy-start(f32[1024,32]{0,1:T(8,128)S(1)} %get-tuple-element.467) | copy-start | bytes 393220
  186.1 66.2 %copy-start.19 = (bf16[512,2048]{1,0:T(8,128)(2,1)S(1)}, bf16[512,2048]{1,0:T(8,128)(2,1)}, u32[]{:S(2)}) copy-start(bf16[512,2048]{1,0:T(8,128)(2,1)} %copy-done.18) | copy-start | bytes 6291460
  253.8 6.7 copy-start.17
  257.1 4.9 copy-start.15
  378.4 3.9 copy-start.22
  378.4 3.9 copy-start.34
  485.5 24.2 %copy-start.23 = (bf16[8,512,4,64]{1,3,2,0:T(8,128)(2,1)}, bf16[8,512,4,64]{1,3,2,0:T(8,128)(2,1)S(1)}, u32[]{:S(2)}) copy-start(bf16[8,512,4,64]{1,3,2,0:T(8,128)(2,1)S(1)} %get-tuple-element.277) | copy-start | bytes 6291460
  560.6 3.2 copy-start.7
  574.9 22.1 %copy-start.2 = (f32[1,1024,4,64]{1,0,3,2:T(1,128)S(1)}, f32[1,1024,4,64]{1,0,3,2:T(1,128)}, u32[]{:S(2)}) copy-start(f32[1,1024,4,64]{1,0,3,2:T(1,128)} %copy.103) | copy-start | bytes 3145732 | tf_op jit(solution)/shard_map/while
  660.6 22.1 %copy-start.2 = (f32[1,1024,4,64]{1,0,3,2:T(1,128)S(1)}, f32[1,1024,4,64]{1,0,3,2:T(1,128)}, u32[]{:S(2)}) copy-start(f32[1,1024,4,64]{1,0,3,2:T(1,128)} %copy.103) | copy-start | bytes 3145732 | tf_op jit(solution)/shard_map/while
  746.4 22.1 %copy-start.2 = (f32[1,1024,4,64]{1,0,3,2:T(1,128)S(1)}, f32[1,1024,4,64]{1,0,3,2:T(1,128)}, u32[]{:S(2)}) copy-start(f32[1,1024,4,64]{1,0,3,2:T(1,128)} %copy.103) | copy-start | bytes 3145732 | tf_op jit(solution)/shard_map/while
  832.2 22.1 %copy-start.2 = (f32[1,1024,4,64]{1,0,3,2:T(1,128)S(1)}, f32[1,1024,4,64]{1,0,3,2:T(1,128)}, u32[]{:S(2)}) copy-start(f32[1,1024,4,64]{1,0,3,2:T(1,128)} %copy.103) | copy-start | bytes 3145732 | tf_op jit(solution)/shard_map/while
  874.4 4.3 copy-start.21
  878.7 40.6 %copy-start.8 = (bf16[32,8,4,1024]{3,1,2,0:T(8,128)(2,1)}, bf16[32,8,4,1024]{3,1,2,0:T(8,128)(2,1)S(1)}, u32[]{:S(2)}) copy-start(bf16[32,8,4,1024]{3,1,2,0:T(8,128)(2,1)S(1)} %copy.97) | copy-start | bytes 6291460
  888.6 17.0 copy-start.12
  888.6 3.9 copy-start.27
  892.5 13.2 copy-start.10
  892.5 13.1 copy-start.29
  905.7 13.6 copy-start.30
  919.3 13.1 copy-start.49
  1017.3 651.5 %reduce-scatter.9.cloned.1.call-start = ((), (), s32[]{:S(2)}) async-start(), calls=%async_computation.14 | async-start | bytes 37748736 | tf_op jit(solution)/shard_map/reduce_scatter | solution.py:133
  1018.9 3.4 copy-start.28
  1022.3 13.4 copy-start.51
  1069.8 645.0 %reduce-scatter.17.cloned.1.call-start = ((), (), s32[]{:S(2)}) async-start(), calls=%async_computation.20 | async-start | bytes 2621440 | tf_op jit(solution)/shard_map/reduce_scatter | solution.py:261
  1081.3 664.4 %reduce-scatter.19.cloned.1.call-start = ((), (), s32[]{:S(2)}) async-start(), calls=%async_computation.21 | async-start | bytes 2621440 | tf_op jit(solution)/shard_map/reduce_scatter | solution.py:263
  1093.9 13.2 copy-start.11
  1094.0 690.5 %reduce-scatter.15.cloned.1.call-start = ((), (), s32[]{:S(2)}) async-start(), calls=%async_computation.19 | async-start | bytes 2621440 | tf_op jit(solution)/shard_map/reduce_scatter | solution.py:260
  1107.1 716.2 %reduce-scatter.13.cloned.1.call-start = ((), (), s32[]{:S(2)}) async-start(), calls=%async_computation.18 | async-start | bytes 2621440 | tf_op jit(solution)/shard_map/reduce_scatter | solution.py:259
  1117.0 796.2 %reduce-scatter.21.cloned.1.call-start = ((), (), s32[]{:S(2)}) async-start(), calls=%async_computation.22 | async-start | bytes 10485760 | tf_op jit(solution)/shard_map/reduce_scatter | solution.py:262
  1141.6 861.9 %reduce-scatter.23.cloned.1.call-start = ((), (), s32[]{:S(2)}) async-start(), calls=%async_computation.23 | async-start | bytes 10485760 | tf_op jit(solution)/shard_map/reduce_scatter | solution.py:264
  1170.5 172.1 %copy-start.1 = (bf16[512,2048]{1,0:T(8,128)(2,1)S(1)}, bf16[512,2048]{1,0:T(8,128)(2,1)}, u32[]{:S(2)}) copy-start(bf16[512,2048]{1,0:T(8,128)(2,1)} %param.23) | copy-start | bytes 6291460
  1170.5 172.1 %copy-start.33 = (f32[2048]{0:T(1024)S(1)}, f32[2048]{0:T(1024)}, u32[]{:S(2)}) copy-start(f32[2048]{0:T(1024)} %copy-done.32) | copy-start | bytes 24580
  1170.5 172.1 %copy-start.36 = (f32[512]{0:T(512)S(1)}, f32[512]{0:T(512)}, u32[]{:S(2)}) copy-start(f32[512]{0:T(512)} %copy-done.35) | copy-start | bytes 6148
  1171.2 174.7 %copy-start.40 = (f32[512]{0:T(512)S(1)}, f32[512]{0:T(512)}, u32[]{:S(2)}) copy-start(f32[512]{0:T(512)} %copy-done.39) | copy-start | bytes 6148
  1171.2 174.8 %copy-start.38 = (f32[512]{0:T(512)S(1)}, f32[512]{0:T(512)}, u32[]{:S(2)}) copy-start(f32[512]{0:T(512)} %copy-done.37) | copy-start | bytes 6148
  1342.6 3.5 copy-start.3
  1714.8 289.3 %copy-start.43 = (f32[2048]{0:T(1024)}, f32[2048]{0:T(1024)S(1)}, u32[]{:S(2)}) copy-start(f32[2048]{0:T(1024)S(1)} %get-tuple-element.893) | copy-start | bytes 24580
  (45 other events, 78.0 us)
Sparse Core Ops, SparseCore 0:
  9.9 29.3 all-gather.10
  41.1 26.6 all-gather.12
  69.6 26.6 all-gather.8
  98.0 52.6 all-gather.16
  152.4 26.4 all-gather.14
  180.3 168.1 all-gather.20
  350.3 51.3 all-gather.18
  403.9 151.0 all-gather.22
  1017.5 325.0 reduce-scatter.10
  1344.9 323.8 reduce-scatter.8
  1672.4 34.3 reduce-scatter.16
  1710.5 35.1 reduce-scatter.18
  1749.2 35.1 reduce-scatter.14
  1788.1 35.1 reduce-scatter.12
  1826.8 86.3 reduce-scatter.20
  1917.1 86.3 reduce-scatter.22
